TPU v7x, 128 devices: a whole 4x4x4 slice. The times are simulated.
128 devices in a mesh: src: 4 (over y), row: 32 (over x, z, core).
Axes of the slice: x: 4, y: 4, z: 4, core: 2. Of those that a mesh axis runs over, the one named last changes fastest.
Arguments:
- load_root: bfloat16 [8192, 1536], P('row', 'src'), may hold values from -48 to 48
- load_branch: bfloat16 [2, 8192, 1536], P(None, 'row', 'src'), may hold values from -48 to 48
- load_leaf: bfloat16 [4, 4096, 1536], P(None, 'row', 'src'), may hold values from -48 to 48
- inverse_root: bfloat16 [8192, 8192], P('row'), may hold values from -1.5 to 1.5, as said below
- inverse_branch: bfloat16 [2, 8192, 8192], P(None, 'row'), may hold values from -1.5 to 1.5, as said below
- inverse_leaf: bfloat16 [4, 4096, 4096], P(None, 'row'), may hold values from -1.5 to 1.5, as said below
- coupling_branch: bfloat16 [2, 2048, 8192], P(None, None, 'row'), may hold values from -0.0625 to 0.0625
- coupling_leaf: bfloat16 [4, 2048, 4096], P(None, None, 'row'), may hold values from -0.09375 to 0.09375
- blocks_branch: int32 [2, 16], replicated, may hold values from 0 to 63, as said below
- blocks_leaf: int32 [4, 16], replicated, may hold values from 0 to 127, as said below
- parents: int32 [4], replicated, may hold values from 0 to 1, as said below
Outputs:
- field_root: float32 [8192, 1536], P('row', 'src')
- field_branch: float32 [2, 8192, 1536], P(None, 'row', 'src')
- field_leaf: float32 [4, 4096, 1536], P(None, 'row', 'src')
- coverage_root: float32 [8192], P('row')
- coverage_branch: float32 [2, 8192], P(None, 'row')
- coverage_leaf: float32 [4, 4096], P(None, 'row')
Inputs may be any that keep to these rules, and one draw needn't show every extreme that they name: `inverse_root`: lower triangular; diagonal entries between 0.5 and 1.5. `inverse_branch`: each block lower triangular; diagonal entries between 0.5 and 1.5. `inverse_leaf`: each block lower triangular; diagonal entries between 0.5 and 1.5. `blocks_branch`: each row holds distinct root block numbers. `blocks_leaf`: each row holds distinct numbers; its first 8 entries are below 8192/128 (parent blocks), the others are 64 or more (root blocks). `parents`: each of the two level-1 separators is the parent of exactly two level-2 separators.
All inputs are finite; a program needn't handle non-finite values.
Results may differ from a plain program's by a relative error of at most 0.0055.
Values may be sent and summed in bfloat16 or wider, within the bound.
A program may use at most 128 MiB of HBM per device.

v0:
```python
import jax
import jax.numpy as jnp
from jax import lax
from jax.sharding import PartitionSpec as P

ROOT_ROWS = 8192
BRANCH_ROWS = 8192
BLOCK_ROWS = 128
COUPLE_BLOCKS = 16


def place_blocks(values, node_ids, blocks, keep_count, first_block, node_total):
    relative = blocks - first_block
    inside = (relative >= 0) & (relative < keep_count)
    target = jnp.where(inside, node_ids * keep_count + relative, node_total * keep_count)
    buckets = jnp.zeros((node_total * keep_count,) + values.shape[1:], jnp.float32)
    buckets = buckets.at[target].add(values, mode="drop")
    return buckets.reshape(node_total, keep_count * values.shape[1], values.shape[2])


def solve_piece(inverse, part_rows):
    return jnp.einsum("nrw,nwc->nrc", inverse, part_rows, preferred_element_type=jnp.float32)


def local(
    load_root,
    load_branch,
    load_leaf,
    inverse_root,
    inverse_branch,
    inverse_leaf,
    coupling_branch,
    coupling_leaf,
    blocks_branch,
    blocks_leaf,
    parents,
):
    row_count = lax.axis_size("row")
    rank_index = lax.axis_index("row")
    source_count = load_leaf.shape[2]
    half_count = COUPLE_BLOCKS // 2
    half_rows = half_count * BLOCK_ROWS
    branch_blocks = BRANCH_ROWS // BLOCK_ROWS
    root_blocks = ROOT_ROWS // BLOCK_ROWS
    root_inverse = inverse_root[None]
    root_load = load_root[None]
    field_leaf = solve_piece(inverse_leaf, lax.all_gather(load_leaf, "row", axis=1, tiled=True))
    leaf_terms = jnp.einsum(
        "nrw,nwc->nrc",
        coupling_leaf,
        field_leaf.astype(jnp.bfloat16),
        preferred_element_type=jnp.float32,
    )
    parent_nodes = jnp.repeat(parents, half_count)
    parent_blocks = blocks_leaf[:, :half_count].reshape(-1)
    upper_blocks = (blocks_leaf[:, half_count:] - branch_blocks).reshape(-1)
    branch_targets = blocks_branch.reshape(-1)
    leaf_total = lax.psum(leaf_terms, "row")
    to_parent = leaf_total[:, :half_rows]
    to_root = leaf_total[:, half_rows:]
    parent_values = to_parent.reshape(-1, BLOCK_ROWS, source_count)
    own_blocks = branch_blocks // row_count
    branch_update = place_blocks(
        parent_values, parent_nodes, parent_blocks, own_blocks, rank_index * own_blocks, 2
    )
    branch_y = (load_branch.astype(jnp.float32) - branch_update).astype(jnp.bfloat16)
    field_branch = solve_piece(inverse_branch, lax.all_gather(branch_y, "row", axis=1, tiled=True))
    branch_terms = jnp.einsum(
        "nrw,nwc->nrc",
        coupling_branch,
        field_branch.astype(jnp.bfloat16),
        preferred_element_type=jnp.float32,
    )
    branch_total = lax.psum(branch_terms, "row")
    root_values = jnp.concatenate(
        [
            to_root.reshape(-1, BLOCK_ROWS, source_count),
            branch_total.reshape(-1, BLOCK_ROWS, source_count),
        ],
        axis=0,
    )
    root_targets = jnp.concatenate([upper_blocks, branch_targets], axis=0)
    root_nodes = jnp.zeros(root_targets.shape, jnp.int32)
    own_root = root_blocks // row_count
    root_update = place_blocks(
        root_values, root_nodes, root_targets, own_root, rank_index * own_root, 1
    )
    root_y = (root_load.astype(jnp.float32) - root_update).astype(jnp.bfloat16)
    field_root = solve_piece(root_inverse, lax.all_gather(root_y, "row", axis=1, tiled=True))
    field_root = field_root[0]
    coverage_root, coverage_branch, coverage_leaf = lax.psum(
        (
            jnp.sum(field_root * field_root, axis=-1),
            jnp.sum(field_branch * field_branch, axis=-1),
            jnp.sum(field_leaf * field_leaf, axis=-1),
        ),
        "src",
    )
    return (field_root, field_branch, field_leaf, coverage_root, coverage_branch, coverage_leaf)


def solution(mesh):
    return jax.shard_map(
        local,
        mesh=mesh,
        in_specs=(
            P("row", "src"),
            P(None, "row", "src"),
            P(None, "row", "src"),
            P("row", None),
            P(None, "row", None),
            P(None, "row", None),
            P(None, None, "row"),
            P(None, None, "row"),
            P(),
            P(),
            P(),
        ),
        out_specs=(
            P("row", "src"),
            P(None, "row", "src"),
            P(None, "row", "src"),
            P("row"),
            P(None, "row"),
            P(None, "row"),
        ),
        check_vma=False,
    )
```

profile of v0, /device:TPU:0, one launch (start us, length us, event | category | flops | bytes accessed | tf_op | source)
XLA Modules:
  0.0 562.4 jit_solution(9774117825941916616)
XLA Ops:
  7.2 0.7 all-gather.5.cloned.1.call-update
  8.0 67.8 %all-gather.5.cloned.1.call-done = bf16[4,4096,384]{2,1,0:T(8,128)(2,1)} async-done(((bf16[4,128,384]{2,1,0:T(8,128)(2,1)}), bf16[4,4096,384]{2,1,0:T(8,128)(2,1)}) %all-gather.5.cloned.1.call-update) | async-done | bytes 12582928 | tf_op jit(solution)/shard_map/all_gather | solution.py:47
  75.8 8.3 %multiply_reduce_fusion = (f32[4,128]{1,0:T(4,128)S(1)}, f32[4,128,384]{2,1,0:T(8,128)S(1)}) fusion(bf16[4,128,4096]{2,1,0:T(8,128)(2,1)} %param.16, bf16[4,4096,384]{2,1,0:T(8,128)(2,1)} %all-gather.5.cloned.1.call-done), kind=kOutput, calls=%fused_computation.7 | convolution fusion | flops 1611005440 | bytes 17565696 | tf_op jit(solution)/shard_map/nrw,nwc->nrc/dot_general | solution.py:22
  84.1 6.3 %convolution_bitcast_fusion = f32[4,2048,384]{1,2,0:T(8,128)} fusion(bf16[4,2048,128]{2,1,0:T(8,128)(2,1)S(1)} %copy-done, f32[4,128,384]{2,1,0:T(8,128)S(1)} %get-tuple-element.30), kind=kOutput, calls=%fused_computation.3 | convolution fusion | flops 805502976 | bytes 15466496 | tf_op jit(solution)/shard_map/nrw,nwc->nrc/dot_general | solution.py:48
  90.5 0.6 copy-done.8
  91.6 131.3 %all-reduce.4.cloned.1.call-done = f32[4,2048,384]{1,2,0:T(8,128)} async-done(((f32[4,2048,384]{1,2,0:T(8,128)}), f32[4,2048,384]{1,2,0:T(8,128)}) %all-reduce.4.cloned.1.call-update) | async-done | bytes 12582928 | tf_op jit(solution)/shard_map/psum | solution.py:58
  223.0 11.8 %fusion.5 = (f32[4,1024,384]{1,2,0:T(8,128)}, f32[4,1024,384]{1,2,0:T(8,128)}) fusion(f32[4,2048,384]{1,2,0:T(8,128)} %all-reduce.4.cloned.1.call-done), kind=kLoop, calls=%fused_computation.25 | loop fusion | bytes 25165824 | tf_op jit(solution)/shard_map/slice | solution.py:60
  234.8 6.6 %copy.24 = f32[4,1024,384]{2,1,0:T(8,128)} copy(f32[4,1024,384]{1,2,0:T(8,128)} %get-tuple-element.22) | data formatting | bytes 12582912 | tf_op jit(solution)/shard_map/slice | solution.py:59
  241.4 9.8 %scatter_fusion = f32[4,128,384]{2,1,0:T(8,128)S(1)} fusion(f32[4,128,384]{2,1,0:T(8,128)S(1)} %broadcast_in_dim.22, s32[32]{0:T(128)S(1)} %fusion.4, f32[32,128,384]{2,1,0:T(8,128)} %bitcast.31), kind=kCustom, calls=%fused_computation | custom fusion | flops 1572864 | bytes 18874496 | tf_op jit(solution)/shard_map/scatter-add | solution.py:17
  251.5 0.8 subtract_convert_fusion
  252.5 69.2 %all-gather.7.cloned.1.call-done = bf16[2,8192,384]{1,2,0:T(8,128)(2,1)} async-done(((bf16[2,256,384]{1,2,0:T(8,128)(2,1)}), bf16[2,8192,384]{1,2,0:T(8,128)(2,1)}) %all-gather.7.cloned.1.call-update) | async-done | bytes 12582928 | tf_op jit(solution)/shard_map/all_gather | solution.py:67
  321.6 11.1 %multiply_reduce_fusion.1 = (f32[2,256]{1,0:T(2,128)S(1)}, f32[2,256,384]{1,2,0:T(8,128)S(1)}) fusion(bf16[2,8192,384]{1,2,0:T(8,128)(2,1)} %all-gather.7.cloned.1.call-done, bf16[2,256,8192]{2,1,0:T(8,128)(2,1)} %param.15), kind=kOutput, calls=%fused_computation.8 | convolution fusion | flops 3221618176 | bytes 21760000 | tf_op jit(solution)/shard_map/nrw,nwc->nrc/dot_general | solution.py:22
  332.7 3.7 convolution_bitcast_fusion.1
  336.4 6.6 %copy.26 = f32[2,2048,384]{2,1,0:T(8,128)} copy(f32[2,2048,384]{1,2,0:T(8,128)} %convolution_bitcast_fusion.1) | data formatting | bytes 12582912 | tf_op jit(solution)/shard_map/nrw,nwc->nrc/dot_general | solution.py:68
  343.8 6.6 %copy.22 = f32[4,1024,384]{2,1,0:T(8,128)} copy(f32[4,1024,384]{1,2,0:T(8,128)} %get-tuple-element.21) | data formatting | bytes 12582912 | tf_op jit(solution)/shard_map/slice | solution.py:60
  350.4 108.2 %all-reduce.6.cloned.1.call-done = f32[32,128,384]{2,1,0:T(8,128)} async-done(((f32[32,128,384]{2,1,0:T(8,128)}), f32[32,128,384]{2,1,0:T(8,128)}) %all-reduce.6.cloned.1.call-update) | async-done | bytes 6291472 | tf_op jit(solution)/shard_map/psum | solution.py:74
  458.6 10.6 %pad_maximum_fusion = f32[64,128,384]{2,1,0:T(8,128)} fusion(f32[32,128,384]{2,1,0:T(8,128)} %all-reduce.6.cloned.1.call-done, f32[32,128,384]{2,1,0:T(8,128)} %bitcast.30), kind=kLoop, calls=%fused_computation.2 | loop fusion | flops 3145728 | bytes 25165824 | tf_op jit(solution)/shard_map/concatenate | solution.py:75
  469.3 19.1 %scatter_fusion.1 = f32[2,128,384]{2,1,0:T(8,128)S(1)} fusion(f32[2,128,384]{2,1,0:T(8,128)S(1)} %broadcast_in_dim.21, s32[64]{0:T(128)S(1)} %fusion.3, f32[64,128,384]{2,1,0:T(8,128)} %pad_maximum_fusion), kind=kCustom, calls=%fused_computation.1 | custom fusion | flops 3145728 | bytes 37748992 | tf_op jit(solution)/shard_map/scatter-add | solution.py:17
  488.4 0.7 fusion
  489.2 1.1 copy.28
  490.3 47.7 %all-gather.9.cloned.1.call-done = bf16[8192,384]{1,0:T(8,128)(2,1)} async-done(((bf16[256,384]{1,0:T(8,128)(2,1)}), bf16[8192,384]{1,0:T(8,128)(2,1)}) %all-gather.9.cloned.1.call-update) | async-done | bytes 6291472 | tf_op jit(solution)/shard_map/all_gather | solution.py:89
  538.0 5.8 %multiply_reduce_fusion.2 = (f32[256]{0:T(256)S(1)}, f32[256,384]{0,1:T(8,128)S(1)}) fusion(bf16[8192,384]{1,0:T(8,128)(2,1)} %all-gather.9.cloned.1.call-done, bf16[256,8192]{1,0:T(8,128)(2,1)} %param.14), kind=kOutput, calls=%fused_computation.12 | convolution fusion | flops 1610809088 | bytes 10880000 | tf_op jit(solution)/shard_map/nrw,nwc->nrc/dot_general | solution.py:22
  543.9 0.9 copy.27
  544.8 11.1 %all-reduce = (f32[256]{0:T(256)}, f32[2,256]{1,0:T(2,128)}, f32[4,128]{1,0:T(4,128)}) all-reduce(f32[256]{0:T(256)S(1)} %get-tuple-element.25, f32[2,256]{1,0:T(2,128)S(1)} %get-tuple-element.27, f32[4,128]{1,0:T(4,128)S(1)} %get-tuple-element.29), channel_id=1, replica_groups=mesh['src'=4,'row'=32] {'src'}, use_global_device_ids=true, to_apply=%region_5.6 | all-reduce | flops 1280 | bytes 10240 | tf_op jit(solution)/shard_map/psum | solution.py:91
  (37 shorter events, 2.0 us)
Async XLA Ops:
  7.2 76.9 %copy-start = (bf16[4,2048,128]{2,1,0:T(8,128)(2,1)S(1)}, bf16[4,2048,128]{2,1,0:T(8,128)(2,1)}, u32[]{:S(2)}) copy-start(bf16[4,2048,128]{2,1,0:T(8,128)(2,1)} %param.18) | copy-start | bytes 6291460
  7.2 68.6 %all-gather.5.cloned.1.call-start = ((), (), s32[]{:S(2)}) async-start(), calls=%async_computation | async-start | bytes 12976128 | tf_op jit(solution)/shard_map/all_gather | solution.py:47
  7.9 215.0 %all-reduce.4.cloned.1.call-start = ((), (), s32[]{:S(2)}) async-start(), calls=%async_computation.1 | async-start | bytes 25165824 | tf_op jit(solution)/shard_map/psum | solution.py:58
  84.1 6.3 %copy-start.2 = (f32[4,128,384]{2,1,0:T(8,128)}, f32[4,128,384]{2,1,0:T(8,128)S(1)}, u32[]{:S(2)}) copy-start(f32[4,128,384]{2,1,0:T(8,128)S(1)} %get-tuple-element.30) | copy-start | bytes 2359300
  90.4 0.7 copy-start.8
  90.4 0.7 copy-start.6
  90.4 1.0 copy-start.4
  90.4 231.2 %all-gather.7.cloned.1.call-start = ((), (), s32[]{:S(2)}) async-start(), calls=%async_computation.2 | async-start | bytes 12976128 | tf_op jit(solution)/shard_map/all_gather | solution.py:67
  252.4 80.3 %copy-start.3 = (bf16[2,2048,256]{2,1,0:T(8,128)(2,1)S(1)}, bf16[2,2048,256]{2,1,0:T(8,128)(2,1)}, u32[]{:S(2)}) copy-start(bf16[2,2048,256]{2,1,0:T(8,128)(2,1)} %param.17) | copy-start | bytes 6291460
  252.4 206.2 %all-reduce.6.cloned.1.call-start = ((), (), s32[]{:S(2)}) async-start(), calls=%async_computation.3 | async-start | bytes 12582912 | tf_op jit(solution)/shard_map/psum | solution.py:74
  342.9 0.7 copy-start.7
  343.0 195.0 %all-gather.9.cloned.1.call-start = ((), (), s32[]{:S(2)}) async-start(), calls=%async_computation.4 | async-start | bytes 6488064 | tf_op jit(solution)/shard_map/all_gather | solution.py:89
  469.3 19.1 %copy-start.5 = (bf16[256,384]{1,0:T(8,128)(2,1)S(1)}, bf16[256,384]{1,0:T(8,128)(2,1)}, u32[]{:S(2)}) copy-start(bf16[256,384]{1,0:T(8,128)(2,1)} %param.11) | copy-start | bytes 589828
  489.2 66.7 %copy-start.1 = (bf16[4,2048,128]{2,1,0:T(8,128)(2,1)S(1)}, bf16[4,2048,128]{2,1,0:T(8,128)(2,1)}, u32[]{:S(2)}) copy-start(bf16[4,2048,128]{2,1,0:T(8,128)(2,1)} %param.18) | copy-start | bytes 6291460
Sparse Core Ops, SparseCore 0:
  10.3 65.4 all-gather.4
  90.6 132.3 all-reduce.3
  252.5 69.0 all-gather.6
  343.1 115.5 all-reduce.5
  489.3 48.6 all-gather.8
where the time goes:
time: 563 us; the launch traced here: 562 us
  waiting for transfers between devices  425 us (75%)
  other arithmetic  41.3 us (7%)
  local copies, waits for them, and re-layouts  35.6 us (6%)
  matrix products  35.2 us (6%)
  between operations  13.9 us (2%)
  blocking collectives  11.1 us (2%)
    psum x1, waiting for transfers between devices, local(): leaf_total = lax.psum(leaf_terms, 'row')  131 us
    psum x1, waiting for transfers between devices, local(): branch_total = lax.psum(branch_terms, 'row')  108 us
    all_gather x1, waiting for transfers between devices, local(): lax.all_gather(branch_y, 'row', axis=1, tiled=True)  69.2 us
    all_gather x1, waiting for transfers between devices, local(): lax.all_gather(load_leaf, 'row', axis=1, tiled=True)  67.8 us
    all_gather x1, waiting for transfers between devices, local(): lax.all_gather(root_y, 'row', axis=1, tiled=True)  47.7 us
    scatter-add x2, other arithmetic, place_blocks(): buckets = buckets.at[target].add(values, mode='drop')  28.9 us
    dot_general x3, matrix products, solve_piece(): jnp.einsum('nrw,nwc->nrc', inverse, part_rows, preferred_element_type=jnp...  25.2 us
    slice x2, local copies, waits for them, and re-layouts, local(): to_root = leaf_total[:, half_rows:]  18.5 us
  transfers between devices with their start and end apart: 5, of which 5 were waited for; matrix products, arithmetic and copies ran while one was open for 1% of the time, Pallas kernels for 0%

commit v1 on v0

--- a/solution.py
+++ b/solution.py
@@ -71,7 +71,11 @@
         field_branch.astype(jnp.bfloat16),
         preferred_element_type=jnp.float32,
     )
-    branch_total = lax.psum(branch_terms, "row")
+    branch_total = branch_terms
+    for hop in (1, 2, 4, 8, 16):
+        branch_total = branch_total + lax.ppermute(
+            branch_total, "row", [(dev, dev ^ hop) for dev in range(32)]
+        )
     root_values = jnp.concatenate(
         [
             to_root.reshape(-1, BLOCK_ROWS, source_count),

time: 563 us -> 1030 us (1.83)
  waiting for transfers between devices: 425 us -> 863 us
  other arithmetic: 41.3 us -> 66.6 us
    ppermute x0 -> x5, waiting for transfers between devices: none -> 546 us  [local(): lax.ppermute(branch_total, 'row', [(dev, dev ^ hop) for dev in range(32)])]
    psum x1 -> x0, waiting for transfers between devices: 108 us -> none  [local(): branch_total = lax.psum(branch_terms, 'row')]
    add x0 -> x5, other arithmetic: none -> 25.4 us  [local(): branch_total + lax.ppermute(branch_total, 'row', [(dev, dev ^ hop) for de...]
  transfers between devices with their start and end apart: 5 -> 9, of which waited for: 5 -> 9; matrix products, arithmetic and copies ran while one was open for 1% -> 1% of each run, Pallas kernels for 0% -> 0%
where the time goes in v1:
time: 1030 us
  waiting for transfers between devices  863 us (84%)
  other arithmetic  66.6 us (6%)
  local copies, waits for them, and re-layouts  35.2 us (3%)
  matrix products  32.6 us (3%)
  between operations  13.9 us (1%)
  blocking collectives  11.1 us (1%)
    ppermute x5, waiting for transfers between devices, local(): lax.ppermute(branch_total, 'row', [(dev, dev ^ hop) for dev in range(32)])  546 us
    psum x1, waiting for transfers between devices, local(): leaf_total = lax.psum(leaf_terms, 'row')  131 us
    all_gather x1, waiting for transfers between devices, local(): lax.all_gather(branch_y, 'row', axis=1, tiled=True)  69.2 us
    all_gather x1, waiting for transfers between devices, local(): lax.all_gather(load_leaf, 'row', axis=1, tiled=True)  67.8 us
    all_gather x1, waiting for transfers between devices, local(): lax.all_gather(root_y, 'row', axis=1, tiled=True)  47.9 us
    scatter-add x2, other arithmetic, place_blocks(): buckets = buckets.at[target].add(values, mode='drop')  28.9 us
    add x5, other arithmetic, local(): branch_total + lax.ppermute(branch_total, 'row', [(dev, dev ^ hop) for de...  25.4 us
    dot_general x3, matrix products, solve_piece(): jnp.einsum('nrw,nwc->nrc', inverse, part_rows, preferred_element_type=jnp...  25.2 us
  transfers between devices with their start and end apart: 9, of which 9 were waited for; matrix products, arithmetic and copies ran while one was open for 1% of the time, Pallas kernels for 0%

profile of v1, /device:TPU:0, one launch (start us, length us, event | category | flops | bytes accessed | tf_op | source)
XLA Modules:
  0.0 1029.5 jit_solution(11038600576329997613)
XLA Ops:
  8.0 67.8 %all-gather.5.cloned.1.call-done = bf16[4,4096,384]{2,1,0:T(8,128)(2,1)} async-done(((bf16[4,128,384]{2,1,0:T(8,128)(2,1)}), bf16[4,4096,384]{2,1,0:T(8,128)(2,1)}) %all-gather.5.cloned.1.call-update) | async-done | bytes 12582928 | tf_op jit(solution)/shard_map/all_gather | solution.py:47
  75.8 8.3 multiply_reduce_fusion
  84.1 6.3 convolution_bitcast_fusion
  91.6 131.3 %all-reduce.3.cloned.1.call-done = f32[4,2048,384]{1,2,0:T(8,128)} async-done(((f32[4,2048,384]{1,2,0:T(8,128)}), f32[4,2048,384]{1,2,0:T(8,128)}) %all-reduce.3.cloned.1.call-update) | async-done | bytes 12582928 | tf_op jit(solution)/shard_map/psum | solution.py:58
  223.0 11.8 %fusion.5 = (f32[4,1024,384]{1,2,0:T(8,128)}, f32[4,1024,384]{1,2,0:T(8,128)}) fusion(f32[4,2048,384]{1,2,0:T(8,128)} %all-reduce.3.cloned.1.call-done), kind=kLoop, calls=%fused_computation.25 | loop fusion | bytes 25165824 | tf_op jit(solution)/shard_map/slice | solution.py:60
  234.8 6.6 copy.24
  241.4 9.8 scatter_fusion
  252.4 69.2 %all-gather.7.cloned.1.call-done = bf16[2,8192,384]{1,2,0:T(8,128)(2,1)} async-done(((bf16[2,256,384]{1,2,0:T(8,128)(2,1)}), bf16[2,8192,384]{1,2,0:T(8,128)(2,1)}) %all-gather.7.cloned.1.call-update) | async-done | bytes 12582928 | tf_op jit(solution)/shard_map/all_gather | solution.py:67
  321.6 11.1 %multiply_reduce_fusion.1 = (f32[2,256]{1,0:T(2,128)S(1)}, f32[2,256,384]{1,2,0:T(8,128)S(1)}) fusion(bf16[2,8192,384]{1,2,0:T(8,128)(2,1)} %all-gather.7.cloned.1.call-done, bf16[2,256,8192]{2,1,0:T(8,128)(2,1)} %param.15), kind=kOutput, calls=%fused_computation.8 | convolution fusion | flops 3221618176 | bytes 21760000 | tf_op jit(solution)/shard_map/nrw,nwc->nrc/dot_general | solution.py:22
  334.2 10.0 collective-permute-done
  344.3 4.1 add.63
  349.6 136.6 %collective-permute-done.1 = f32[2,2048,384]{1,2,0:T(8,128)} collective-permute-done((f32[2,2048,384]{1,2,0:T(8,128)S(1)}, f32[2,2048,384]{1,2,0:T(8,128)}, u32[]{:S(2)}, u32[]{:S(2)}) %collective-permute-start.1) | collective-permute-done | bytes 6291488 | tf_op jit(solution)/shard_map/ppermute | solution.py:76
  492.5 136.3 %collective-permute-done.2 = f32[2,2048,384]{1,2,0:T(8,128)} collective-permute-done((f32[2,2048,384]{1,2,0:T(8,128)S(1)}, f32[2,2048,384]{1,2,0:T(8,128)}, u32[]{:S(2)}, u32[]{:S(2)}) %collective-permute-start.2) | collective-permute-done | bytes 6291488 | tf_op jit(solution)/shard_map/ppermute | solution.py:76
  628.8 4.1 add.65
  634.1 134.8 %collective-permute-done.3 = f32[2,2048,384]{1,2,0:T(8,128)S(1)} collective-permute-done((f32[2,2048,384]{1,2,0:T(8,128)S(1)}, f32[2,2048,384]{1,2,0:T(8,128)S(1)}, u32[]{:S(2)}, u32[]{:S(2)}) %collective-permute-start.3) | collective-permute-done | bytes 6291488 | tf_op jit(solution)/shard_map/ppermute | solution.py:76
  775.1 6.6 copy.22
  781.7 128.1 %collective-permute-done.4 = f32[2,2048,384]{1,2,0:T(8,128)} collective-permute-done((f32[2,2048,384]{1,2,0:T(8,128)}, f32[2,2048,384]{1,2,0:T(8,128)}, u32[]{:S(2)}, u32[]{:S(2)}) %collective-permute-start.4) | collective-permute-done | bytes 6291488 | tf_op jit(solution)/shard_map/ppermute | solution.py:76
  909.8 9.2 add.67
  919.0 6.6 copy.26
  925.5 10.6 %pad_maximum_fusion = f32[64,128,384]{2,1,0:T(8,128)} fusion(f32[32,128,384]{2,1,0:T(8,128)} %bitcast.31, f32[32,128,384]{2,1,0:T(8,128)} %bitcast.29), kind=kLoop, calls=%fused_computation.2 | loop fusion | flops 3145728 | bytes 25165824 | tf_op jit(solution)/shard_map/concatenate | solution.py:79
  936.2 19.1 %scatter_fusion.1 = f32[2,128,384]{2,1,0:T(8,128)S(1)} fusion(f32[2,128,384]{2,1,0:T(8,128)S(1)} %broadcast_in_dim.21, s32[64]{0:T(128)S(1)} %fusion.3, f32[64,128,384]{2,1,0:T(8,128)} %pad_maximum_fusion), kind=kCustom, calls=%fused_computation.1 | custom fusion | flops 3145728 | bytes 37748992 | tf_op jit(solution)/shard_map/scatter-add | solution.py:17
  957.2 47.9 %all-gather.9.cloned.1.call-done = bf16[8192,384]{1,0:T(8,128)(2,1)} async-done(((bf16[256,384]{1,0:T(8,128)(2,1)}), bf16[8192,384]{1,0:T(8,128)(2,1)}) %all-gather.9.cloned.1.call-update) | async-done | bytes 6291472 | tf_op jit(solution)/shard_map/all_gather | solution.py:93
  1005.1 5.8 multiply_reduce_fusion.2
  1011.9 11.1 %all-reduce = (f32[256]{0:T(256)}, f32[2,256]{1,0:T(2,128)}, f32[4,128]{1,0:T(4,128)}) all-reduce(f32[256]{0:T(256)S(1)} %get-tuple-element.25, f32[2,256]{1,0:T(2,128)S(1)} %get-tuple-element.27, f32[4,128]{1,0:T(4,128)S(1)} %get-tuple-element.29), channel_id=1, replica_groups=mesh['src'=4,'row'=32] {'src'}, use_global_device_ids=true, to_apply=%region_4.5 | all-reduce | flops 1280 | bytes 10240 | tf_op jit(solution)/shard_map/psum | solution.py:95
  (49 shorter events, 22.5 us)
Async XLA Ops:
  7.2 76.9 %copy-start = (bf16[4,2048,128]{2,1,0:T(8,128)(2,1)S(1)}, bf16[4,2048,128]{2,1,0:T(8,128)(2,1)}, u32[]{:S(2)}) copy-start(bf16[4,2048,128]{2,1,0:T(8,128)(2,1)} %param.18) | copy-start | bytes 6291460
  7.2 68.6 %all-gather.5.cloned.1.call-start = ((), (), s32[]{:S(2)}) async-start(), calls=%async_computation | async-start | bytes 12976128 | tf_op jit(solution)/shard_map/all_gather | solution.py:47
  7.9 215.0 %all-reduce.3.cloned.1.call-start = ((), (), s32[]{:S(2)}) async-start(), calls=%async_computation.1 | async-start | bytes 25165824 | tf_op jit(solution)/shard_map/psum | solution.py:58
  84.1 6.3 copy-start.2
  90.4 0.7 copy-start.8
  90.4 0.7 copy-start.6
  90.4 1.0 copy-start.4
  90.4 231.1 %all-gather.7.cloned.1.call-start = ((), (), s32[]{:S(2)}) async-start(), calls=%async_computation.2 | async-start | bytes 12976128 | tf_op jit(solution)/shard_map/all_gather | solution.py:67
  252.4 80.3 %copy-start.3 = (bf16[2,2048,256]{2,1,0:T(8,128)(2,1)S(1)}, bf16[2,2048,256]{2,1,0:T(8,128)(2,1)}, u32[]{:S(2)}) copy-start(bf16[2,2048,256]{2,1,0:T(8,128)(2,1)} %param.17) | copy-start | bytes 6291460
  252.4 752.7 %all-gather.9.cloned.1.call-start = ((), (), s32[]{:S(2)}) async-start(), calls=%async_computation.3 | async-start | bytes 6488064 | tf_op jit(solution)/shard_map/all_gather | solution.py:93
  333.7 10.6 %collective-permute-start = (f32[2,2048,384]{1,2,0:T(8,128)S(1)}, f32[2,2048,384]{1,2,0:T(8,128)}, u32[]{:S(2)}, u32[]{:S(2)}) collective-permute-start(f32[2,2048,384]{1,2,0:T(8,128)S(1)} %convolution_bitcast_fusion.1), channel_id=1, source_target_pairs={{0,1},{1,0},{2,3},{3,2},{4,5},{5,4},{6,7},{7,6},{8,9},{9,8},{10,11... | collective-permute-start | bytes 18874376 | tf_op jit(solution)/shard_map/ppermute | solution.py:76
  348.3 137.9 %collective-permute-start.1 = (f32[2,2048,384]{1,2,0:T(8,128)S(1)}, f32[2,2048,384]{1,2,0:T(8,128)}, u32[]{:S(2)}, u32[]{:S(2)}) collective-permute-start(f32[2,2048,384]{1,2,0:T(8,128)S(1)} %add.63), channel_id=1, source_target_pairs={{0,2},{1,3},{2,0},{3,1},{4,6},{5,7},{6,4},{7,5},{8,10},{9,11},{10,... | collective-permute-start | bytes 18874376 | tf_op jit(solution)/shard_map/ppermute | solution.py:76
  490.3 138.5 %collective-permute-start.2 = (f32[2,2048,384]{1,2,0:T(8,128)S(1)}, f32[2,2048,384]{1,2,0:T(8,128)}, u32[]{:S(2)}, u32[]{:S(2)}) collective-permute-start(f32[2,2048,384]{1,2,0:T(8,128)S(1)} %add.64), channel_id=1, source_target_pairs={{0,4},{1,5},{2,6},{3,7},{4,0},{5,1},{6,2},{7,3},{8,12},{9,13},{10,... | collective-permute-start | bytes 18874376 | tf_op jit(solution)/shard_map/ppermute | solution.py:76
  632.9 142.1 %copy-start.7 = (s32[2,16]{1,0:T(2,128)S(1)}, s32[2,16]{1,0:T(2,128)}, u32[]{:S(2)}) copy-start(s32[2,16]{1,0:T(2,128)} %param.19) | copy-start | bytes 388
  632.9 136.0 %collective-permute-start.3 = (f32[2,2048,384]{1,2,0:T(8,128)S(1)}, f32[2,2048,384]{1,2,0:T(8,128)S(1)}, u32[]{:S(2)}, u32[]{:S(2)}) collective-permute-start(f32[2,2048,384]{1,2,0:T(8,128)S(1)} %add.65), channel_id=1, source_target_pairs={{0,8},{1,9},{2,10},{3,11},{4,12},{5,13},{6,14},{7,15},{8,0},{9,1},... | collective-permute-start | bytes 18874376 | tf_op jit(solution)/shard_map/ppermute | solution.py:76
  772.9 136.9 %collective-permute-start.4 = (f32[2,2048,384]{1,2,0:T(8,128)}, f32[2,2048,384]{1,2,0:T(8,128)}, u32[]{:S(2)}, u32[]{:S(2)}) collective-permute-start(f32[2,2048,384]{1,2,0:T(8,128)} %add.66), channel_id=1, source_target_pairs={{0,16},{1,17},{2,18},{3,19},{4,20},{5,21},{6,22},{7,23},{8,24},{9,... | collective-permute-start | bytes 18874376 | tf_op jit(solution)/shard_map/ppermute | solution.py:76
  936.2 19.1 %copy-start.5 = (bf16[256,384]{1,0:T(8,128)(2,1)S(1)}, bf16[256,384]{1,0:T(8,128)(2,1)}, u32[]{:S(2)}) copy-start(bf16[256,384]{1,0:T(8,128)(2,1)} %param.11) | copy-start | bytes 589828
  956.0 67.0 %copy-start.1 = (bf16[4,2048,128]{2,1,0:T(8,128)(2,1)S(1)}, bf16[4,2048,128]{2,1,0:T(8,128)(2,1)}, u32[]{:S(2)}) copy-start(bf16[4,2048,128]{2,1,0:T(8,128)(2,1)} %param.18) | copy-start | bytes 6291460
Sparse Core Ops, SparseCore 0:
  10.3 65.4 all-gather.4
  90.6 132.3 all-reduce.2
  252.5 69.0 all-gather.6
  956.2 48.9 all-gather.8
